TPU v7x, 32 devices: a whole 2x2x4 slice. The times are simulated.
32 devices in a mesh: shard: 4 (over z), ctx: 2 (over core), tp: 4 (over y, x).
Axes of the slice: x: 2, y: 2, z: 4, core: 2. Of those that a mesh axis runs over, the one named last changes fastest.
Arguments:
- tokens: bfloat16 [8, 2048, 768], P('shard', 'ctx'), may hold values from -6 to 6
- segment_ids: int32 [8, 2048], P('shard', 'ctx'), may hold values from 0 to 34, as said below
- offsets: int32 [8, 2048], P('shard', 'ctx'), may hold values from 0 to 799, as said below
- qkv_weight: bfloat16 [768, 3, 768], P(('shard', 'ctx'), None, 'tp'), may hold values from -0.3125 to 0.3125
- out_weight: bfloat16 [768, 768], P(('shard', 'ctx'), 'tp'), may hold values from -0.875 to 0.875
- ffn_weight: bfloat16 [768, 2, 3072], P(('shard', 'ctx'), None, 'tp'), may hold values from -0.21875 to 0.21875
- qkv_bias: float32 [3, 768], P(None, 'tp'), may hold values from -3 to 3
- ffn_bias: float32 [3072], P('tp'), may hold values from -3 to 3
- norm_gain: float32 [2, 768], replicated, may hold values from 0.5 to 1.5
- shift_params: float32 [4, 768], replicated, may hold values from -3 to 3
- out_grad: bfloat16 [8, 2048, 768], P('shard', 'ctx'), may hold values from -6 to 6
Outputs:
- outputs: bfloat16 [8, 2048, 768], P('shard', 'ctx')
- grad_tokens: bfloat16 [8, 2048, 768], P('shard', 'ctx')
- grad_qkv_weight: float32 [768, 3, 768], P(('shard', 'ctx'), None, 'tp')
- grad_out_weight: float32 [768, 768], P(('shard', 'ctx'), 'tp')
- grad_ffn_weight: float32 [768, 2, 3072], P(('shard', 'ctx'), None, 'tp')
- grad_qkv_bias: float32 [3, 768], P(None, 'tp')
- grad_ffn_bias: float32 [3072], P('tp')
- grad_norm_gain: float32 [2, 768], replicated
- grad_shift_params: float32 [4, 768], replicated
Inputs may be any that keep to these rules, and one draw needn't show every extreme that they name: `segment_ids`: segment numbers start at 0 in each sequence and rise by one where a new document begins. offsets are 0 at a document's first token and rise by one along it; a document has at most 800 tokens, and every document but a sequence's last has at least 60.
All inputs are finite; a program needn't handle non-finite values.
Results may differ from a plain program's by a relative error of at most 0.017.
The roundings to bfloat16 on the way count: a program that leaves them out, or rounds other values in their place, can miss the bound.
Values may be sent and summed in bfloat16 or wider, within the bound.
No kernel may reach another device: no remote copies, remote signals or barrier semaphores. Data moves between devices by JAX's collectives and lax.ppermute only.
A program may use at most 192 MiB of HBM per device.

v0:
```python
from functools import partial
import jax
import jax.numpy as jnp
from jax import lax
from jax.sharding import PartitionSpec as P

HEAD = 64
EPSILON = 1e-12


def rotate_pairs(values, offsets, direction):
    half_size = values.shape[-1] // 2
    frequency = 10000.0 ** (-2.0 * jnp.arange(half_size, dtype=jnp.float32) / values.shape[-1])
    angles = offsets.astype(jnp.float32)[:, None] * frequency[None, :]
    cosine = jnp.cos(angles)[:, None, :]
    sine_part = direction * jnp.sin(angles)[:, None, :]
    paired = values.reshape(values.shape[:-1] + (half_size, 2))
    even_part = paired[..., 0]
    odd_part = paired[..., 1]
    turned = jnp.stack(
        [even_part * cosine - odd_part * sine_part, even_part * sine_part + odd_part * cosine],
        axis=-1,
    )
    return turned.reshape(values.shape)


def norm_parts(rows_in):
    centre = rows_in - jnp.mean(rows_in, axis=-1, keepdims=True)
    inverse_root = lax.rsqrt(jnp.mean(centre * centre, axis=-1, keepdims=True) + EPSILON)
    return (centre * inverse_root, inverse_root)


def norm_back(grad_in, scaled, inverse_root, gain_row):
    grad_scaled = grad_in * gain_row
    term_mean = jnp.mean(grad_scaled, axis=-1, keepdims=True)
    term_along = jnp.mean(grad_scaled * scaled, axis=-1, keepdims=True)
    return inverse_root * (grad_scaled - term_mean - scaled * term_along)


def attention_weights(qkv_weight, out_weight):
    return (
        lax.all_gather(qkv_weight, ("shard", "ctx"), axis=0, tiled=True),
        lax.all_gather(out_weight, ("shard", "ctx"), axis=0, tiled=True),
    )


def feed_weights(ffn_weight):
    return lax.all_gather(ffn_weight, ("shard", "ctx"), axis=0, tiled=True)


def masked_scores(queries, keys_all, same_doc, score_scale):
    scores = (
        jnp.einsum("shd,thd->hst", queries, keys_all, preferred_element_type=jnp.float32)
        * score_scale
    )
    return jnp.where(same_doc, scores, -1e30)


def contract_last(left, right):
    return lax.dot_general(
        left, right, (((1,), (1,)), ((), ())), preferred_element_type=jnp.float32
    )


def contract_first(left, right):
    return lax.dot_general(
        left, right, (((0,), (0,)), ((), ())), preferred_element_type=jnp.float32
    )


def body(
    tokens,
    segment_ids,
    offsets,
    qkv_weight,
    out_weight,
    ffn_weight,
    qkv_bias,
    ffn_bias,
    norm_gain,
    shift_params,
    out_grad,
):
    model_width = tokens.shape[2]
    part_width = qkv_weight.shape[2]
    hidden_width = ffn_weight.shape[2]
    local_heads = part_width // HEAD
    score_scale = HEAD ** (-0.5)
    tp_count = lax.axis_size("tp")
    tp_rank = lax.axis_index("tp")

    def micro_step(totals, micro_batch):
        tokens_mb, segment_mb, offsets_mb, grad_mb = micro_batch
        half_len = tokens_mb.shape[0]
        share_len = half_len // tp_count
        share_start = tp_rank * share_len

        def share_rows(rows):
            return lax.dynamic_slice_in_dim(rows, share_start, share_len, 0)

        qkv_full, out_full = attention_weights(qkv_weight, out_weight)
        ffn_full = feed_weights(ffn_weight)
        projected = (
            jnp.einsum("sd,dke->kse", tokens_mb, qkv_full, preferred_element_type=jnp.float32)
            + qkv_bias[:, None, :]
        )
        per_head = projected.reshape(3, half_len, local_heads, HEAD)
        queries = rotate_pairs(per_head[0], offsets_mb, 1.0).astype(jnp.bfloat16)
        keys_own = rotate_pairs(per_head[1], offsets_mb, 1.0).astype(jnp.bfloat16)
        values_own = per_head[2].astype(jnp.bfloat16)
        pair_own = jnp.stack([keys_own, values_own]).reshape(2, half_len, part_width)
        segment_own = segment_mb.astype(jnp.bfloat16)
        pair_all, segment_all = (
            lax.all_gather(pair_own, "ctx", axis=1, tiled=True),
            lax.all_gather(segment_own, "ctx", axis=0, tiled=True),
        )
        seq_len = pair_all.shape[1]
        keys_all = pair_all[0].reshape(seq_len, local_heads, HEAD)
        values_all = pair_all[1].reshape(seq_len, local_heads, HEAD)
        same_doc = (segment_own[:, None] == segment_all[None, :])[None]
        scores = masked_scores(queries, keys_all, same_doc, score_scale)
        row_top = jnp.max(scores, axis=-1, keepdims=True)
        exponent = jnp.exp(scores - row_top)
        row_total = jnp.sum(exponent, axis=-1, keepdims=True)
        probs_b = (exponent / row_total).astype(jnp.bfloat16)
        log_total = row_top + jnp.log(row_total)
        context = jnp.einsum(
            "hst,thd->shd", probs_b, values_all, preferred_element_type=jnp.float32
        )
        context = context.reshape(half_len, part_width).astype(jnp.bfloat16)
        attended = lax.psum(contract_last(context, out_full), "tp")
        first_scaled, first_root = norm_parts(
            tokens_mb.astype(jnp.float32) + attended + shift_params[2]
        )
        normed = first_scaled * norm_gain[0] + shift_params[0]
        normed_b = normed.astype(jnp.bfloat16)
        hidden_in = (
            jnp.dot(normed_b, ffn_full[:, 0, :], preferred_element_type=jnp.float32) + ffn_bias
        )
        activated, gelu_pull = jax.vjp(partial(jax.nn.gelu, approximate=False), hidden_in)
        activated_b = activated.astype(jnp.bfloat16)
        returned = lax.psum(contract_last(activated_b, ffn_full[:, 1, :]), "tp")
        second_scaled, second_root = norm_parts(normed + returned + shift_params[3])
        layer_out = (second_scaled * norm_gain[1] + shift_params[1]).astype(jnp.bfloat16)
        qkv_back, out_back = attention_weights(qkv_weight, out_weight)
        ffn_back = feed_weights(ffn_weight)
        grad_top = grad_mb.astype(jnp.float32)
        grad_gain_two = jnp.sum(share_rows(grad_top) * share_rows(second_scaled), axis=0)
        grad_second = norm_back(grad_top, second_scaled, second_root, norm_gain[1])
        grad_second_b = grad_second.astype(jnp.bfloat16)
        grad_down = contract_first(grad_second_b, activated_b)
        grad_act = jnp.dot(grad_second_b, ffn_back[:, 1, :], preferred_element_type=jnp.float32)
        grad_hidden = gelu_pull(grad_act)[0].astype(jnp.bfloat16)
        grad_up = contract_first(normed_b, grad_hidden)
        grad_ffn_bias = jnp.sum(grad_hidden.astype(jnp.float32), axis=0)
        ffn_part = contract_last(grad_hidden, ffn_back[:, 0, :])
        grad_normed = grad_second + lax.psum(ffn_part, "tp")
        grad_first = norm_back(grad_normed, first_scaled, first_root, norm_gain[0])
        grad_first_b = grad_first.astype(jnp.bfloat16)
        normed_part = share_rows(grad_normed)
        first_part = share_rows(grad_first)
        grad_gain_one = jnp.sum(normed_part * share_rows(first_scaled), axis=0)
        grad_out_proj = contract_first(grad_first_b, context)
        grad_context = jnp.dot(grad_first_b, out_back, preferred_element_type=jnp.float32).astype(
            jnp.bfloat16
        )
        grad_context = grad_context.reshape(half_len, local_heads, HEAD)
        scores_again = masked_scores(queries, keys_all, same_doc, score_scale)
        probs = jnp.exp(scores_again - log_total)
        probs_again = probs.astype(jnp.bfloat16)
        grad_probs = jnp.einsum(
            "shd,thd->hst", grad_context, values_all, preferred_element_type=jnp.float32
        )
        row_dot = jnp.sum(probs * grad_probs, axis=-1, keepdims=True)
        grad_scores = (probs * (grad_probs - row_dot)).astype(jnp.bfloat16)
        grad_queries = (
            jnp.einsum("hst,thd->shd", grad_scores, keys_all, preferred_element_type=jnp.float32)
            * score_scale
        )
        grad_keys = (
            jnp.einsum("hst,shd->thd", grad_scores, queries, preferred_element_type=jnp.float32)
            * score_scale
        )
        grad_values = jnp.einsum(
            "hst,shd->thd", probs_again, grad_context, preferred_element_type=jnp.float32
        )
        grad_pair = lax.psum_scatter(
            jnp.stack([grad_keys, grad_values]).reshape(2, seq_len, part_width),
            "ctx",
            scatter_dimension=1,
            tiled=True,
        )
        grad_pair = grad_pair.reshape(2, half_len, local_heads, HEAD)
        grad_proj = jnp.stack(
            [
                rotate_pairs(grad_queries, offsets_mb, -1.0),
                rotate_pairs(grad_pair[0], offsets_mb, -1.0),
                grad_pair[1],
            ]
        )
        grad_proj = grad_proj.reshape(3, half_len, part_width).astype(jnp.bfloat16)
        grad_qkv_bias = jnp.sum(grad_proj.astype(jnp.float32), axis=1)
        grad_qkv = jnp.einsum(
            "sd,kse->dke", tokens_mb, grad_proj, preferred_element_type=jnp.float32
        )
        grad_branch = jnp.einsum(
            "kse,dke->sd", grad_proj, qkv_back, preferred_element_type=jnp.float32
        )
        grad_inputs = (grad_first + lax.psum(grad_branch, "tp")).astype(jnp.bfloat16)
        grad_shift = jnp.stack(
            [
                jnp.sum(normed_part, axis=0),
                jnp.sum(share_rows(grad_top), axis=0),
                jnp.sum(first_part, axis=0),
                jnp.sum(share_rows(grad_second), axis=0),
            ]
        )
        grad_gain = jnp.stack([grad_gain_one, grad_gain_two])
        grad_ffn = jnp.stack([grad_up, grad_down], axis=1)
        updated = (
            totals[0] + grad_qkv,
            totals[1] + grad_out_proj,
            totals[2] + grad_ffn,
            totals[3] + grad_qkv_bias,
            totals[4] + grad_ffn_bias,
            totals[5] + grad_gain,
            totals[6] + grad_shift,
        )
        return (updated, (layer_out, grad_inputs))

    zero_grads = (
        jnp.zeros((model_width, 3, part_width), jnp.float32),
        jnp.zeros((model_width, part_width), jnp.float32),
        jnp.zeros((model_width, 2, hidden_width), jnp.float32),
        jnp.zeros((3, part_width), jnp.float32),
        jnp.zeros((hidden_width,), jnp.float32),
        jnp.zeros((2, model_width), jnp.float32),
        jnp.zeros((4, model_width), jnp.float32),
    )
    totals, (outputs, grad_tokens) = lax.scan(
        micro_step, zero_grads, (tokens, segment_ids, offsets, out_grad)
    )
    grad_qkv_weight, grad_out_weight, grad_ffn_weight = (
        lax.psum_scatter(totals[0], ("shard", "ctx"), scatter_dimension=0, tiled=True),
        lax.psum_scatter(totals[1], ("shard", "ctx"), scatter_dimension=0, tiled=True),
        lax.psum_scatter(totals[2], ("shard", "ctx"), scatter_dimension=0, tiled=True),
    )
    placed_qkv = lax.dynamic_update_slice(
        jnp.zeros((3, part_width * tp_count), jnp.float32),
        totals[3],
        (jnp.int32(0), tp_rank * part_width),
    )
    placed_ffn = lax.dynamic_update_slice(
        jnp.zeros((hidden_width * tp_count,), jnp.float32), totals[4], (tp_rank * hidden_width,)
    )
    summed_qkv, summed_ffn, grad_norm_gain, grad_shift_params = lax.psum(
        (placed_qkv, placed_ffn, totals[5], totals[6]), ("shard", "ctx", "tp")
    )
    grad_qkv_bias = lax.dynamic_slice_in_dim(summed_qkv, tp_rank * part_width, part_width, 1)
    grad_ffn_bias = lax.dynamic_slice_in_dim(summed_ffn, tp_rank * hidden_width, hidden_width, 0)
    return (
        outputs,
        grad_tokens,
        grad_qkv_weight,
        grad_out_weight,
        grad_ffn_weight,
        grad_qkv_bias,
        grad_ffn_bias,
        grad_norm_gain,
        grad_shift_params,
    )


def solution(mesh):
    return jax.shard_map(
        body,
        mesh=mesh,
        in_specs=(
            P("shard", "ctx", None),
            P("shard", "ctx"),
            P("shard", "ctx"),
            P(("shard", "ctx"), None, "tp"),
            P(("shard", "ctx"), "tp"),
            P(("shard", "ctx"), None, "tp"),
            P(None, "tp"),
            P("tp"),
            P(),
            P(),
            P("shard", "ctx", None),
        ),
        out_specs=(
            P("shard", "ctx", None),
            P("shard", "ctx", None),
            P(("shard", "ctx"), None, "tp"),
            P(("shard", "ctx"), "tp"),
            P(("shard", "ctx"), None, "tp"),
            P(None, "tp"),
            P("tp"),
            P(),
            P(),
        ),
        check_vma=False,
    )
```

profile of v0, /device:TPU:0, one launch (start us, length us, event | category | flops | bytes accessed | tf_op | source)
XLA Modules:
  0.0 1406.7 jit_solution(18068525269604240569)
XLA Ops:
  10.9 1200.5 %while.29 = (s32[]{:T(128)}, f32[768,3,192]{0,2,1:T(8,128)}, f32[768,192]{0,1:T(8,128)}, f32[768,2,768]{2,0,1:T(8,128)}, f32[3,192]{1,0:T(4,128)}, /*index=5*/f3...) while((s32[]{:T(128)}, f32[768,3,192]{0,2,1:T(8,128)}, ...), condition=%wide.region_25.26_spmd.clone, body=%wide.region_0.25_spmd.clone.sunk | while | flops 15947476992 | bytes 964769600 | solution.py:240
  10.9 23.1 %all_gather.42 = bf16[768,3,192]{2,1,0:T(4,128)(2,1)} all-gather(bf16[96,3,192]{2,1,0:T(4,128)(2,1)S(1)} %get-tuple-element.828), channel_id=1, replica_groups=mesh['shard'=4,'ctx'=2,'tp'=4] {'shard','ctx'}, dimensions={0}, use_global_device_ids=true | all-gather | bytes 995328 | tf_op jit(solution)/shard_map/while/body/eval_jaxpr/all_gather | solution.py:42
  63.8 16.3 %all_gather.41 = bf16[768,192]{1,0:T(8,128)(2,1)} all-gather(bf16[96,192]{1,0:T(8,128)(2,1)} %get-tuple-element.832), channel_id=1, replica_groups=mesh['shard'=4,'ctx'=2,'tp'=4] {'shard','ctx'}, dimensions={0}, use_global_device_ids=true | all-gather | bytes 331776 | tf_op jit(solution)/shard_map/while/body/eval_jaxpr/all_gather | solution.py:43
  122.3 84.8 %all-reduce.10.cloned.1.call-done = f32[1024,768]{1,0:T(8,128)} async-done(((f32[1024,768]{1,0:T(8,128)}), f32[1024,768]{1,0:T(8,128)}) %all-reduce.10.cloned.1.call-update) | async-done | bytes 3145744 | tf_op jit(solution)/shard_map/while/body/eval_jaxpr/psum | solution.py:131
  228.0 87.1 %all-reduce.12.cloned.1.call-done = f32[1024,768]{1,0:T(8,128)} async-done(((f32[1024,768]{1,0:T(8,128)}), f32[1024,768]{1,0:T(8,128)}) %all-reduce.12.cloned.1.call-update) | async-done | bytes 3145744 | tf_op jit(solution)/shard_map/while/body/eval_jaxpr/psum | solution.py:142
  335.9 86.1 %all-reduce.14.cloned.1.call-done = f32[1024,768]{1,0:T(8,128)} async-done(((f32[1024,768]{1,0:T(8,128)}), f32[1024,768]{1,0:T(8,128)}) %all-reduce.14.cloned.1.call-update) | async-done | bytes 3145744 | tf_op jit(solution)/shard_map/while/body/eval_jaxpr/psum | solution.py:157
  430.4 11.4 fusion.160
  441.8 16.4 %multiply_reduce_fusion.14 = (f32[3,1024]{1,0:T(4,128)}, f32[3,1024,2048]{2,1,0:T(8,128)}) fusion(f32[3,1024,2048]{2,1,0:T(8,128)} %get-tuple-element.731, f32[3,1024]{1,0:T(4,128)S(1)} %log_add_fusion.2, bf16[1024,3,64]{0,2,1:T(8,128)(2,1)} %bitcast.223, bf16[2048,3,64]{0,2,1:T(8,128)(2,1)} %bitcast.227), kind=kOutput, calls=%fused_computation.1.clone.1 | convolution fusion | flops 824177664 | bytes 51535872 | tf_op jit(solution)/shard_map/while/body/eval_jaxpr/shd,thd->hst/dot_general | solution.py:171
  458.2 16.8 %multiply_convert_fusion.5 = bf16[3,1024,2048]{2,1,0:T(8,128)(2,1)S(1)} fusion(f32[3,1024,2048]{2,1,0:T(8,128)} %get-tuple-element.750, f32[3,1024,2048]{2,1,0:T(8,128)} %get-tuple-element.731, f32[3,1024]{1,0:T(4,128)} %get-tuple-element.751, f32[3,1024]{1,0:T(4,128)S(1)} %log_add_fusion.2), kind=kLoop, calls=%fused_computation.clone.1 | loop fusion | flops 25165824 | bytes 62939136 | tf_op jit(solution)/shard_map/while/body/eval_jaxpr/convert_element_type | solution.py:175
  536.2 70.3 %all-reduce.16.cloned.1.call-done = f32[1024,768]{1,0:T(8,128)} async-done(((f32[1024,768]{1,0:T(8,128)}), f32[1024,768]{1,0:T(8,128)}) %all-reduce.16.cloned.1.call-update) | async-done | bytes 3145744 | tf_op jit(solution)/shard_map/while/body/eval_jaxpr/psum | solution.py:209
  610.1 21.4 %all_gather.42 = bf16[768,3,192]{2,1,0:T(4,128)(2,1)} all-gather(bf16[96,3,192]{2,1,0:T(4,128)(2,1)S(1)} %get-tuple-element.828), channel_id=1, replica_groups=mesh['shard'=4,'ctx'=2,'tp'=4] {'shard','ctx'}, dimensions={0}, use_global_device_ids=true | all-gather | bytes 995328 | tf_op jit(solution)/shard_map/while/body/eval_jaxpr/all_gather | solution.py:42
  661.3 16.0 %all_gather.41 = bf16[768,192]{1,0:T(8,128)(2,1)} all-gather(bf16[96,192]{1,0:T(8,128)(2,1)} %get-tuple-element.832), channel_id=1, replica_groups=mesh['shard'=4,'ctx'=2,'tp'=4] {'shard','ctx'}, dimensions={0}, use_global_device_ids=true | all-gather | bytes 331776 | tf_op jit(solution)/shard_map/while/body/eval_jaxpr/all_gather | solution.py:43
  719.7 83.5 %all-reduce.10.cloned.1.call-done = f32[1024,768]{1,0:T(8,128)} async-done(((f32[1024,768]{1,0:T(8,128)}), f32[1024,768]{1,0:T(8,128)}) %all-reduce.10.cloned.1.call-update) | async-done | bytes 3145744 | tf_op jit(solution)/shard_map/while/body/eval_jaxpr/psum | solution.py:131
  808.3 11.2 multiply_convert_fusion.4
  824.1 87.2 %all-reduce.12.cloned.1.call-done = f32[1024,768]{1,0:T(8,128)} async-done(((f32[1024,768]{1,0:T(8,128)}), f32[1024,768]{1,0:T(8,128)}) %all-reduce.12.cloned.1.call-update) | async-done | bytes 3145744 | tf_op jit(solution)/shard_map/while/body/eval_jaxpr/psum | solution.py:142
  931.9 86.4 %all-reduce.14.cloned.1.call-done = f32[1024,768]{1,0:T(8,128)} async-done(((f32[1024,768]{1,0:T(8,128)}), f32[1024,768]{1,0:T(8,128)}) %all-reduce.14.cloned.1.call-update) | async-done | bytes 3145744 | tf_op jit(solution)/shard_map/while/body/eval_jaxpr/psum | solution.py:157
  1026.6 11.4 fusion.160
  1038.0 16.4 %multiply_reduce_fusion.14 = (f32[3,1024]{1,0:T(4,128)}, f32[3,1024,2048]{2,1,0:T(8,128)}) fusion(f32[3,1024,2048]{2,1,0:T(8,128)} %get-tuple-element.731, f32[3,1024]{1,0:T(4,128)S(1)} %log_add_fusion.2, bf16[1024,3,64]{0,2,1:T(8,128)(2,1)} %bitcast.223, bf16[2048,3,64]{0,2,1:T(8,128)(2,1)} %bitcast.227), kind=kOutput, calls=%fused_computation.1.clone.1 | convolution fusion | flops 824177664 | bytes 51535872 | tf_op jit(solution)/shard_map/while/body/eval_jaxpr/shd,thd->hst/dot_general | solution.py:171
  1054.4 16.8 %multiply_convert_fusion.5 = bf16[3,1024,2048]{2,1,0:T(8,128)(2,1)S(1)} fusion(f32[3,1024,2048]{2,1,0:T(8,128)} %get-tuple-element.750, f32[3,1024,2048]{2,1,0:T(8,128)} %get-tuple-element.731, f32[3,1024]{1,0:T(4,128)} %get-tuple-element.751, f32[3,1024]{1,0:T(4,128)S(1)} %log_add_fusion.2), kind=kLoop, calls=%fused_computation.clone.1 | loop fusion | flops 25165824 | bytes 62939136 | tf_op jit(solution)/shard_map/while/body/eval_jaxpr/convert_element_type | solution.py:175
  1134.2 68.6 %all-reduce.16.cloned.1.call-done = f32[1024,768]{1,0:T(8,128)} async-done(((f32[1024,768]{1,0:T(8,128)}), f32[1024,768]{1,0:T(8,128)}) %all-reduce.16.cloned.1.call-update) | async-done | bytes 3145744 | tf_op jit(solution)/shard_map/while/body/eval_jaxpr/psum | solution.py:209
  1225.5 42.1 %all-reduce.1 = (f32[3,768]{1,0:T(4,128)S(1)}, f32[3072]{0:T(1024)S(1)}, f32[2,768]{1,0:T(2,128)}, f32[4,768]{1,0:T(4,128)}) all-reduce(f32[3,768]{1,0:T(4,128)S(1)} %dynamic_update_slice.19, f32[3072]{0:T(1024)S(1)} %dynamic_update_slice.20, ...), channel_id=1, replica_groups=mesh['shard'=4,'ctx'=2,'tp'=4] {'shard','ctx','tp'}, use_global_device_ids=true, to_apply=%region_29.30 | all-reduce | flops 9984 | bytes 79872 | tf_op jit(solution)/shard_map/psum | solution.py:256
  1270.2 56.7 %all-reduce.8.cloned.1.call-done = f32[768,2,768]{2,1,0:T(2,128)} async-done(((f32[768,2,768]{2,1,0:T(2,128)}), f32[768,2,768]{2,1,0:T(2,128)}) %all-reduce.8.cloned.1.call-update) | async-done | bytes 4718608
  1328.8 32.5 %reduce-scatter.6.cloned.1.call-done = f32[96,192]{1,0:T(8,128)} async-done(((f32[768,192]{1,0:T(8,128)}), f32[96,192]{1,0:T(8,128)}) %reduce-scatter.6.cloned.1.call-update) | async-done | bytes 73744 | tf_op jit(solution)/shard_map/reduce_scatter | solution.py:245
  1361.3 37.6 %reduce-scatter.4.cloned.1.call-done = f32[96,3,192]{2,0,1:T(8,128)} async-done(((f32[768,3,192]{2,0,1:T(8,128)}), f32[96,3,192]{2,0,1:T(8,128)}) %reduce-scatter.4.cloned.1.call-update) | async-done | bytes 221200 | tf_op jit(solution)/shard_map/reduce_scatter | solution.py:244
  (527 shorter events, 382.8 us)
Async XLA Ops:
  10.9 71.7 %all-gather.7.cloned.1.call-start = ((), (), s32[]{:S(2)}) async-start(), calls=%async_computation.6 | async-start | bytes 2359296 | tf_op jit(solution)/shard_map/while/body/eval_jaxpr/all_gather | solution.py:114
  57.9 149.1 %all-reduce.10.cloned.1.call-start = ((), (), s32[]{:S(2)}) async-start(), calls=%async_computation.7 | async-start | bytes 6291456 | tf_op jit(solution)/shard_map/while/body/eval_jaxpr/psum | solution.py:131
  119.9 92.2 %all-gather.9.cloned.1.call-start = ((), (), s32[]{:S(2)}) async-start(), calls=%async_computation.8 | async-start | bytes 2654208 | tf_op jit(solution)/shard_map/while/body/eval_jaxpr/all_gather | solution.py:48
  120.5 194.6 %all-reduce.12.cloned.1.call-start = ((), (), s32[]{:S(2)}) async-start(), calls=%async_computation.9 | async-start | bytes 6291456 | tf_op jit(solution)/shard_map/while/body/eval_jaxpr/psum | solution.py:142
  120.8 194.3 %copy-start.35 = (f32[768]{0:T(1024)}, f32[768]{0:T(1024)S(1)}, u32[]{:S(2)}) copy-start(f32[768]{0:T(1024)S(1)} %get-tuple-element.733) | copy-start | bytes 9220 | tf_op jit(solution)/shard_map/while
  122.3 192.8 %copy-start.45 = (f32[768]{0:T(1024)}, f32[768]{0:T(1024)S(1)}, u32[]{:S(2)}) copy-start(f32[768]{0:T(1024)S(1)} %get-tuple-element.737) | copy-start | bytes 9220 | tf_op jit(solution)/shard_map/while
  227.7 87.4 %copy-start.48 = (f32[768]{0:T(1024)S(1)}, f32[768]{0:T(1024)}, u32[]{:S(2)}) copy-start(f32[768]{0:T(1024)} %get-tuple-element.736) | copy-start | bytes 9220 | tf_op jit(solution)/shard_map/while
  227.7 194.3 %all-reduce.14.cloned.1.call-start = ((), (), s32[]{:S(2)}) async-start(), calls=%async_computation.10 | async-start | bytes 6291456 | tf_op jit(solution)/shard_map/while/body/eval_jaxpr/psum | solution.py:157
  334.7 163.7 %reduce-scatter.8.cloned.1.call-start = ((), (), s32[]{:S(2)}) async-start(), calls=%async_computation.11 | async-start | bytes 4718592 | tf_op jit(solution)/shard_map/while/body/eval_jaxpr/reduce_scatter | solution.py:187
  481.7 124.7 %all-reduce.16.cloned.1.call-start = ((), (), s32[]{:S(2)}) async-start(), calls=%async_computation.12 | async-start | bytes 6291456 | tf_op jit(solution)/shard_map/while/body/eval_jaxpr/psum | solution.py:209
  610.0 69.7 %all-gather.7.cloned.1.call-start = ((), (), s32[]{:S(2)}) async-start(), calls=%async_computation.6 | async-start | bytes 2359296 | tf_op jit(solution)/shard_map/while/body/eval_jaxpr/all_gather | solution.py:114
  655.4 147.8 %all-reduce.10.cloned.1.call-start = ((), (), s32[]{:S(2)}) async-start(), calls=%async_computation.7 | async-start | bytes 6291456 | tf_op jit(solution)/shard_map/while/body/eval_jaxpr/psum | solution.py:131
  717.1 91.2 %all-gather.9.cloned.1.call-start = ((), (), s32[]{:S(2)}) async-start(), calls=%async_computation.8 | async-start | bytes 2654208 | tf_op jit(solution)/shard_map/while/body/eval_jaxpr/all_gather | solution.py:48
  717.7 193.6 %all-reduce.12.cloned.1.call-start = ((), (), s32[]{:S(2)}) async-start(), calls=%async_computation.9 | async-start | bytes 6291456 | tf_op jit(solution)/shard_map/while/body/eval_jaxpr/psum | solution.py:142
  718.2 193.0 %copy-start.35 = (f32[768]{0:T(1024)}, f32[768]{0:T(1024)S(1)}, u32[]{:S(2)}) copy-start(f32[768]{0:T(1024)S(1)} %get-tuple-element.733) | copy-start | bytes 9220 | tf_op jit(solution)/shard_map/while
  719.7 191.5 %copy-start.45 = (f32[768]{0:T(1024)}, f32[768]{0:T(1024)S(1)}, u32[]{:S(2)}) copy-start(f32[768]{0:T(1024)S(1)} %get-tuple-element.737) | copy-start | bytes 9220 | tf_op jit(solution)/shard_map/while
  823.9 87.4 %copy-start.48 = (f32[768]{0:T(1024)S(1)}, f32[768]{0:T(1024)}, u32[]{:S(2)}) copy-start(f32[768]{0:T(1024)} %get-tuple-element.736) | copy-start | bytes 9220 | tf_op jit(solution)/shard_map/while
  823.9 194.3 %all-reduce.14.cloned.1.call-start = ((), (), s32[]{:S(2)}) async-start(), calls=%async_computation.10 | async-start | bytes 6291456 | tf_op jit(solution)/shard_map/while/body/eval_jaxpr/psum | solution.py:157
  930.8 163.7 %reduce-scatter.8.cloned.1.call-start = ((), (), s32[]{:S(2)}) async-start(), calls=%async_computation.11 | async-start | bytes 4718592 | tf_op jit(solution)/shard_map/while/body/eval_jaxpr/reduce_scatter | solution.py:187
  1077.9 125.0 %all-reduce.16.cloned.1.call-start = ((), (), s32[]{:S(2)}) async-start(), calls=%async_computation.12 | async-start | bytes 6291456 | tf_op jit(solution)/shard_map/while/body/eval_jaxpr/psum | solution.py:209
  1131.0 71.9 %copy-start.3 = (f32[1024,768]{1,0:T(8,128)S(1)}, f32[1024,768]{1,0:T(8,128)}, u32[]{:S(2)}) copy-start(f32[1024,768]{1,0:T(8,128)} %copy-done.1) | copy-start | bytes 9437188 | tf_op jit(solution)/shard_map/while
  1211.3 115.6 %all-reduce.8.cloned.1.call-start = ((), (), s32[]{:S(2)}) async-start(), calls=%async_computation.5 | async-start | bytes 9437184
  1219.5 141.8 %reduce-scatter.6.cloned.1.call-start = ((), (), s32[]{:S(2)}) async-start(), calls=%async_computation.4 | async-start | bytes 884736 | tf_op jit(solution)/shard_map/reduce_scatter | solution.py:245
  1221.8 177.1 %reduce-scatter.4.cloned.1.call-start = ((), (), s32[]{:S(2)}) async-start(), calls=%async_computation.3 | async-start | bytes 2654208 | tf_op jit(solution)/shard_map/reduce_scatter | solution.py:244
  (139 other events, 747.8 us)
Sparse Core Ops, SparseCore 0:
  58.0 9.4 all-gather.6
  120.0 86.9 all-reduce.9
  227.8 87.2 all-reduce.11
  334.8 87.1 all-reduce.13
  481.9 10.8 reduce-scatter.7
  519.3 87.1 all-reduce.15
  655.5 8.5 all-gather.6
  717.2 85.9 all-reduce.9
  824.0 87.2 all-reduce.11
  931.0 87.2 all-reduce.13
  1078.1 10.8 reduce-scatter.7
  1115.7 87.1 all-reduce.15
Sparse Core Ops, SparseCore 1:
  122.6 31.1 all-gather.8
  719.7 30.1 all-gather.8
  1219.6 107.2 all-reduce.7
  1329.8 31.5 reduce-scatter.5
  1364.3 34.5 reduce-scatter.3
where the time goes:
time: 1410 us
  waiting for transfers between devices  782 us (55%)
  matrix products  197 us (14%)
  other arithmetic  160 us (11%)
  blocking collectives  123 us (9%)
  local copies, waits for them, and re-layouts  119 us (8%)
  between operations  16.7 us (1%)
    psum x2, waiting for transfers between devices, micro_step(): returned = lax.psum(contract_last(activated_b, ffn_full[:, 1, :]), 'tp')  174 us
    psum x2, waiting for transfers between devices, micro_step(): grad_normed = grad_second + lax.psum(ffn_part, 'tp')  172 us
    psum x2, waiting for transfers between devices, micro_step(): attended = lax.psum(contract_last(context, out_full), 'tp')  168 us
    psum x2, waiting for transfers between devices, micro_step(): lax.psum(grad_branch, 'tp')  139 us
    unnamed x4, waiting for transfers between devices  56.7 us
    all_gather x2, blocking collectives, attention_weights(): lax.all_gather(qkv_weight, ('shard', 'ctx'), axis=0, tiled=True)  44.4 us
    while x280, local copies, waits for them, and re-layouts  43.6 us
    psum x1, blocking collectives, body(): lax.psum((placed_qkv, placed_ffn, totals[5], totals[6]), ('shard', 'ctx',...  42.1 us
  transfers between devices with their start and end apart: 17, of which 11 were waited for; matrix products, arithmetic and copies ran while one was open for 7% of the time, Pallas kernels for 0%

commit v1 on v0

--- a/solution.py
+++ b/solution.py
@@ -38,9 +38,34 @@
 
 
 def attention_weights(qkv_weight, out_weight):
+
+    def update_indices_now(mine):
+        newest = lax.axis_size(("shard", "ctx"))
+        e_now = lax.axis_index(("shard", "ctx"))
+        carry, lower, e_next = (newest, e_now, mine.shape[0])
+        entries = tuple(
+            (dev_i * carry if tick == 0 else dev_i for tick, dev_i in enumerate(mine.shape))
+        )
+        y1 = jnp.zeros(entries, mine.dtype)
+        out_arr = lax.dynamic_update_slice_in_dim(y1, mine, lower * e_next, axis=0)
+        b_now = w1 = mine
+        for at in range(1, carry // 2 + 1):
+            fresh = tuple(((tick, (tick + 1) % carry) for tick in range(carry)))
+            b_now = lax.ppermute(b_now, axis_name=("shard", "ctx"), perm=fresh)
+            out_arr = lax.dynamic_update_slice_in_dim(
+                out_arr, b_now, (lower - at) % carry * e_next, axis=0
+            )
+            if 2 * at < carry:
+                part_next = tuple(((tick, (tick - 1) % carry) for tick in range(carry)))
+                w1 = lax.ppermute(w1, axis_name=("shard", "ctx"), perm=part_next)
+                out_arr = lax.dynamic_update_slice_in_dim(
+                    out_arr, w1, (lower + at) % carry * e_next, axis=0
+                )
+        return out_arr
+
     return (
         lax.all_gather(qkv_weight, ("shard", "ctx"), axis=0, tiled=True),
-        lax.all_gather(out_weight, ("shard", "ctx"), axis=0, tiled=True),
+        update_indices_now(out_weight),
     )
 
 

time: 1410 us -> 1420 us (level)
  blocking collectives: 123 us -> 86.9 us
  local copies, waits for them, and re-layouts: 119 us -> 144 us
    all_gather x2 -> x0, blocking collectives: 32.2 us -> none  [attention_weights(): lax.all_gather(out_weight, ('shard', 'ctx'), axis=0, tiled=True)]
    dynamic_update_slice x0 -> x16, local copies, waits for them, and re-layouts: none -> 22.7 us  [the longest x8 11.3 us: update_indices_now(): lax.dynamic_update_slice_in_dim(out_arr, b_now, (lower - at) % carry * e_...]
    while x280 -> x272, local copies, waits for them, and re-layouts: 43.6 us -> 43.5 us
  transfers between devices with their start and end apart: 17 -> 24, of which waited for: 11 -> 15; matrix products, arithmetic and copies ran while one was open for 7% -> 9% of each run, Pallas kernels for 0% -> 0%
where the time goes in v1:
time: 1420 us
  waiting for transfers between devices  790 us (56%)
  matrix products  200 us (14%)
  other arithmetic  160 us (11%)
  local copies, waits for them, and re-layouts  144 us (10%)
  blocking collectives  86.9 us (6%)
  between operations  16.7 us (1%)
    psum x2, waiting for transfers between devices, micro_step(): returned = lax.psum(contract_last(activated_b, ffn_full[:, 1, :]), 'tp')  174 us
    psum x2, waiting for transfers between devices, micro_step(): grad_normed = grad_second + lax.psum(ffn_part, 'tp')  172 us
    psum x2, waiting for transfers between devices, micro_step(): attended = lax.psum(contract_last(context, out_full), 'tp')  168 us
    psum x2, waiting for transfers between devices, micro_step(): lax.psum(grad_branch, 'tp')  139 us
    unnamed x4, waiting for transfers between devices  56.7 us
    while x272, local copies, waits for them, and re-layouts  43.5 us
    psum x1, blocking collectives, body(): lax.psum((placed_qkv, placed_ffn, totals[5], totals[6]), ('shard', 'ctx',...  42.1 us
    all_gather x2, blocking collectives, attention_weights(): lax.all_gather(qkv_weight, ('shard', 'ctx'), axis=0, tiled=True)  40.2 us
  transfers between devices with their start and end apart: 24, of which 15 were waited for; matrix products, arithmetic and copies ran while one was open for 9% of the time, Pallas kernels for 0%

profile of v1, /device:TPU:0, one launch (start us, length us, event | category | flops | bytes accessed | tf_op | source)
XLA Modules:
  0.0 1419.4 jit_solution(9439125175515305674)
XLA Ops:
  31.7 1192.3 %while.29 = (s32[]{:T(128)}, f32[768,3,192]{0,2,1:T(8,128)}, f32[768,192]{0,1:T(8,128)}, f32[768,2,768]{2,0,1:T(8,128)}, f32[3,192]{1,0:T(4,128)}, /*index=5*/f3...) while((s32[]{:T(128)}, f32[768,3,192]{0,2,1:T(8,128)}, ...), condition=%wide.region_25.26_spmd.clone, body=%wide.region_0.25_spmd.clone.sunk | while | flops 15947476992 | bytes 963161344 | solution.py:265
  31.7 18.8 %all_gather.32 = bf16[768,3,192]{2,1,0:T(4,128)(2,1)} all-gather(bf16[96,3,192]{2,1,0:T(4,128)(2,1)S(1)} %get-tuple-element.1010), channel_id=1, replica_groups=mesh['shard'=4,'ctx'=2,'tp'=4] {'shard','ctx'}, dimensions={0}, use_global_device_ids=true | all-gather | bytes 995328 | tf_op jit(solution)/shard_map/while/body/eval_jaxpr/all_gather | solution.py:67
  136.1 84.7 %all-reduce.10.cloned.1.call-done = f32[1024,768]{1,0:T(8,128)} async-done(((f32[1024,768]{1,0:T(8,128)}), f32[1024,768]{1,0:T(8,128)}) %all-reduce.10.cloned.1.call-update) | async-done | bytes 3145744 | tf_op jit(solution)/shard_map/while/body/eval_jaxpr/psum | solution.py:156
  225.9 11.2 multiply_convert_fusion.4
  241.7 87.1 %all-reduce.12.cloned.1.call-done = f32[1024,768]{1,0:T(8,128)} async-done(((f32[1024,768]{1,0:T(8,128)}), f32[1024,768]{1,0:T(8,128)}) %all-reduce.12.cloned.1.call-update) | async-done | bytes 3145744 | tf_op jit(solution)/shard_map/while/body/eval_jaxpr/psum | solution.py:167
  349.5 86.1 %all-reduce.14.cloned.1.call-done = f32[1024,768]{1,0:T(8,128)} async-done(((f32[1024,768]{1,0:T(8,128)}), f32[1024,768]{1,0:T(8,128)}) %all-reduce.14.cloned.1.call-update) | async-done | bytes 3145744 | tf_op jit(solution)/shard_map/while/body/eval_jaxpr/psum | solution.py:182
  445.0 11.4 fusion.165
  456.4 16.5 %multiply_reduce_fusion.14 = (f32[3,1024]{1,0:T(4,128)}, f32[3,1024,2048]{2,1,0:T(8,128)}) fusion(f32[3,1024,2048]{2,1,0:T(8,128)} %get-tuple-element.871, f32[3,1024]{1,0:T(4,128)S(1)} %log_add_fusion.2, bf16[1024,3,64]{0,2,1:T(8,128)(2,1)} %bitcast.223, bf16[2048,3,64]{0,2,1:T(8,128)(2,1)} %bitcast.227), kind=kOutput, calls=%fused_computation.1.clone.1 | convolution fusion | flops 824177664 | bytes 51535872 | tf_op jit(solution)/shard_map/while/body/eval_jaxpr/shd,thd->hst/dot_general | solution.py:196
  473.0 16.8 %multiply_convert_fusion.5 = bf16[3,1024,2048]{2,1,0:T(8,128)(2,1)S(1)} fusion(f32[3,1024,2048]{2,1,0:T(8,128)} %get-tuple-element.890, f32[3,1024,2048]{2,1,0:T(8,128)} %get-tuple-element.871, f32[3,1024]{1,0:T(4,128)} %get-tuple-element.891, f32[3,1024]{1,0:T(4,128)S(1)} %log_add_fusion.2), kind=kLoop, calls=%fused_computation.clone.1 | loop fusion | flops 25165824 | bytes 62939136 | tf_op jit(solution)/shard_map/while/body/eval_jaxpr/convert_element_type | solution.py:200
  550.8 70.2 %all-reduce.16.cloned.1.call-done = f32[1024,768]{1,0:T(8,128)} async-done(((f32[1024,768]{1,0:T(8,128)}), f32[1024,768]{1,0:T(8,128)}) %all-reduce.16.cloned.1.call-update) | async-done | bytes 3145744 | tf_op jit(solution)/shard_map/while/body/eval_jaxpr/psum | solution.py:234
  624.8 21.4 %all_gather.32 = bf16[768,3,192]{2,1,0:T(4,128)(2,1)} all-gather(bf16[96,3,192]{2,1,0:T(4,128)(2,1)S(1)} %get-tuple-element.1010), channel_id=1, replica_groups=mesh['shard'=4,'ctx'=2,'tp'=4] {'shard','ctx'}, dimensions={0}, use_global_device_ids=true | all-gather | bytes 995328 | tf_op jit(solution)/shard_map/while/body/eval_jaxpr/all_gather | solution.py:67
  692.8 11.0 fusion.155
  731.6 83.4 %all-reduce.10.cloned.1.call-done = f32[1024,768]{1,0:T(8,128)} async-done(((f32[1024,768]{1,0:T(8,128)}), f32[1024,768]{1,0:T(8,128)}) %all-reduce.10.cloned.1.call-update) | async-done | bytes 3145744 | tf_op jit(solution)/shard_map/while/body/eval_jaxpr/psum | solution.py:156
  820.2 11.2 multiply_convert_fusion.4
  835.9 87.2 %all-reduce.12.cloned.1.call-done = f32[1024,768]{1,0:T(8,128)} async-done(((f32[1024,768]{1,0:T(8,128)}), f32[1024,768]{1,0:T(8,128)}) %all-reduce.12.cloned.1.call-update) | async-done | bytes 3145744 | tf_op jit(solution)/shard_map/while/body/eval_jaxpr/psum | solution.py:167
  943.6 86.3 %all-reduce.14.cloned.1.call-done = f32[1024,768]{1,0:T(8,128)} async-done(((f32[1024,768]{1,0:T(8,128)}), f32[1024,768]{1,0:T(8,128)}) %all-reduce.14.cloned.1.call-update) | async-done | bytes 3145744 | tf_op jit(solution)/shard_map/while/body/eval_jaxpr/psum | solution.py:182
  1039.2 11.4 fusion.165
  1050.6 16.5 %multiply_reduce_fusion.14 = (f32[3,1024]{1,0:T(4,128)}, f32[3,1024,2048]{2,1,0:T(8,128)}) fusion(f32[3,1024,2048]{2,1,0:T(8,128)} %get-tuple-element.871, f32[3,1024]{1,0:T(4,128)S(1)} %log_add_fusion.2, bf16[1024,3,64]{0,2,1:T(8,128)(2,1)} %bitcast.223, bf16[2048,3,64]{0,2,1:T(8,128)(2,1)} %bitcast.227), kind=kOutput, calls=%fused_computation.1.clone.1 | convolution fusion | flops 824177664 | bytes 51535872 | tf_op jit(solution)/shard_map/while/body/eval_jaxpr/shd,thd->hst/dot_general | solution.py:196
  1067.2 16.8 %multiply_convert_fusion.5 = bf16[3,1024,2048]{2,1,0:T(8,128)(2,1)S(1)} fusion(f32[3,1024,2048]{2,1,0:T(8,128)} %get-tuple-element.890, f32[3,1024,2048]{2,1,0:T(8,128)} %get-tuple-element.871, f32[3,1024]{1,0:T(4,128)} %get-tuple-element.891, f32[3,1024]{1,0:T(4,128)S(1)} %log_add_fusion.2), kind=kLoop, calls=%fused_computation.clone.1 | loop fusion | flops 25165824 | bytes 62939136 | tf_op jit(solution)/shard_map/while/body/eval_jaxpr/convert_element_type | solution.py:200
  1146.9 68.6 %all-reduce.16.cloned.1.call-done = f32[1024,768]{1,0:T(8,128)} async-done(((f32[1024,768]{1,0:T(8,128)}), f32[1024,768]{1,0:T(8,128)}) %all-reduce.16.cloned.1.call-update) | async-done | bytes 3145744 | tf_op jit(solution)/shard_map/while/body/eval_jaxpr/psum | solution.py:234
  1239.5 42.1 %all-reduce.1 = (f32[3,768]{1,0:T(4,128)S(1)}, f32[3072]{0:T(1024)S(1)}, f32[2,768]{1,0:T(2,128)}, f32[4,768]{1,0:T(4,128)}) all-reduce(f32[3,768]{1,0:T(4,128)S(1)} %dynamic_update_slice.75, f32[3072]{0:T(1024)S(1)} %dynamic_update_slice.76, ...), channel_id=1, replica_groups=mesh['shard'=4,'ctx'=2,'tp'=4] {'shard','ctx','tp'}, use_global_device_ids=true, to_apply=%region_29.30 | all-reduce | flops 9984 | bytes 79872 | tf_op jit(solution)/shard_map/psum | solution.py:281
  1282.9 56.6 %all-reduce.8.cloned.1.call-done = f32[768,2,768]{2,1,0:T(2,128)} async-done(((f32[768,2,768]{2,1,0:T(2,128)}), f32[768,2,768]{2,1,0:T(2,128)}) %all-reduce.8.cloned.1.call-update) | async-done | bytes 4718608
  1341.5 32.5 %reduce-scatter.6.cloned.1.call-done = f32[96,192]{1,0:T(8,128)} async-done(((f32[768,192]{1,0:T(8,128)}), f32[96,192]{1,0:T(8,128)}) %reduce-scatter.6.cloned.1.call-update) | async-done | bytes 73744 | tf_op jit(solution)/shard_map/reduce_scatter | solution.py:270
  1374.0 37.6 %reduce-scatter.4.cloned.1.call-done = f32[96,3,192]{2,0,1:T(8,128)} async-done(((f32[768,3,192]{2,0,1:T(8,128)}), f32[96,3,192]{2,0,1:T(8,128)}) %reduce-scatter.4.cloned.1.call-update) | async-done | bytes 221200 | tf_op jit(solution)/shard_map/reduce_scatter | solution.py:269
  (555 shorter events, 409.8 us)
Async XLA Ops:
  8.0 6.5 collective-permute-start
  8.5 6.7 collective-permute-start.1
  15.2 5.4 collective-permute-start.2
  15.2 5.4 collective-permute-start.3
  20.6 5.4 collective-permute-start.4
  21.2 7.6 collective-permute-start.5
  26.0 5.7 collective-permute-start.6
  31.7 63.9 %all-gather.7.cloned.1.call-start = ((), (), s32[]{:S(2)}) async-start(), calls=%async_computation.6 | async-start | bytes 2359296 | tf_op jit(solution)/shard_map/while/body/eval_jaxpr/all_gather | solution.py:139
  74.4 146.5 %all-reduce.10.cloned.1.call-start = ((), (), s32[]{:S(2)}) async-start(), calls=%async_computation.7 | async-start | bytes 6291456 | tf_op jit(solution)/shard_map/while/body/eval_jaxpr/psum | solution.py:156
  133.8 92.2 %all-gather.9.cloned.1.call-start = ((), (), s32[]{:S(2)}) async-start(), calls=%async_computation.8 | async-start | bytes 2654208 | tf_op jit(solution)/shard_map/while/body/eval_jaxpr/all_gather | solution.py:73
  134.3 194.5 %all-reduce.12.cloned.1.call-start = ((), (), s32[]{:S(2)}) async-start(), calls=%async_computation.9 | async-start | bytes 6291456 | tf_op jit(solution)/shard_map/while/body/eval_jaxpr/psum | solution.py:167
  241.4 194.2 %all-reduce.14.cloned.1.call-start = ((), (), s32[]{:S(2)}) async-start(), calls=%async_computation.10 | async-start | bytes 6291456 | tf_op jit(solution)/shard_map/while/body/eval_jaxpr/psum | solution.py:182
  348.3 164.8 %reduce-scatter.8.cloned.1.call-start = ((), (), s32[]{:S(2)}) async-start(), calls=%async_computation.11 | async-start | bytes 4718592 | tf_op jit(solution)/shard_map/while/body/eval_jaxpr/reduce_scatter | solution.py:212
  496.5 124.6 %all-reduce.16.cloned.1.call-start = ((), (), s32[]{:S(2)}) async-start(), calls=%async_computation.12 | async-start | bytes 6291456 | tf_op jit(solution)/shard_map/while/body/eval_jaxpr/psum | solution.py:234
  624.7 66.1 %all-gather.7.cloned.1.call-start = ((), (), s32[]{:S(2)}) async-start(), calls=%async_computation.6 | async-start | bytes 2359296 | tf_op jit(solution)/shard_map/while/body/eval_jaxpr/all_gather | solution.py:139
  670.0 145.1 %all-reduce.10.cloned.1.call-start = ((), (), s32[]{:S(2)}) async-start(), calls=%async_computation.7 | async-start | bytes 6291456 | tf_op jit(solution)/shard_map/while/body/eval_jaxpr/psum | solution.py:156
  729.0 91.1 %all-gather.9.cloned.1.call-start = ((), (), s32[]{:S(2)}) async-start(), calls=%async_computation.8 | async-start | bytes 2654208 | tf_op jit(solution)/shard_map/while/body/eval_jaxpr/all_gather | solution.py:73
  729.6 193.4 %all-reduce.12.cloned.1.call-start = ((), (), s32[]{:S(2)}) async-start(), calls=%async_computation.9 | async-start | bytes 6291456 | tf_op jit(solution)/shard_map/while/body/eval_jaxpr/psum | solution.py:167
  835.7 194.2 %all-reduce.14.cloned.1.call-start = ((), (), s32[]{:S(2)}) async-start(), calls=%async_computation.10 | async-start | bytes 6291456 | tf_op jit(solution)/shard_map/while/body/eval_jaxpr/psum | solution.py:182
  942.5 164.8 %reduce-scatter.8.cloned.1.call-start = ((), (), s32[]{:S(2)}) async-start(), calls=%async_computation.11 | async-start | bytes 4718592 | tf_op jit(solution)/shard_map/while/body/eval_jaxpr/reduce_scatter | solution.py:212
  1090.7 124.8 %all-reduce.16.cloned.1.call-start = ((), (), s32[]{:S(2)}) async-start(), calls=%async_computation.12 | async-start | bytes 6291456 | tf_op jit(solution)/shard_map/while/body/eval_jaxpr/psum | solution.py:234
  1224.0 115.6 %all-reduce.8.cloned.1.call-start = ((), (), s32[]{:S(2)}) async-start(), calls=%async_computation.5 | async-start | bytes 9437184
  1232.2 141.8 %reduce-scatter.6.cloned.1.call-start = ((), (), s32[]{:S(2)}) async-start(), calls=%async_computation.4 | async-start | bytes 884736 | tf_op jit(solution)/shard_map/reduce_scatter | solution.py:270
  1234.4 177.1 %reduce-scatter.4.cloned.1.call-start = ((), (), s32[]{:S(2)}) async-start(), calls=%async_computation.3 | async-start | bytes 2654208 | tf_op jit(solution)/shard_map/reduce_scatter | solution.py:269
  (145 other events, 1697.7 us)
Sparse Core Ops, SparseCore 0:
  74.5 9.5 all-gather.6
  133.9 86.9 all-reduce.9
  241.6 87.2 all-reduce.11
  348.5 87.1 all-reduce.13
  496.6 10.8 reduce-scatter.7
  533.9 87.1 all-reduce.15
  670.1 8.5 all-gather.6
  729.1 85.9 all-reduce.9
  835.8 87.2 all-reduce.11
  942.7 87.1 all-reduce.13
  1090.8 10.8 reduce-scatter.7
  1128.4 87.1 all-reduce.15
Sparse Core Ops, SparseCore 1:
  136.4 31.1 all-gather.8
  731.7 30.1 all-gather.8
  1232.3 107.2 all-reduce.7
  1342.4 31.5 reduce-scatter.5
  1377.0 34.5 reduce-scatter.3
